TPU v7x, 32 devices: a whole 2x2x4 slice. The times are simulated.
32 devices in a mesh: seg: 4 (over z), mpo: 4 (over x, core), sec: 2 (over y).
Axes of the slice: x: 2, y: 2, z: 4, core: 2. Of those that a mesh axis runs over, the one named last changes fastest.
Arguments:
- state: bfloat16 [4, 1024, 1024], P('seg', 'sec'), may hold values from -6 to 6
- left_env: bfloat16 [4, 12, 1024, 1024], P('seg', 'mpo', 'sec'), may hold values from -0.1875 to 0.1875
- right_env: bfloat16 [4, 12, 1024, 1024], P('seg', 'mpo'), may hold values from -0.1875 to 0.1875
- inv_singular: float32 [4, 1024], P('seg'), may hold values from 0.5 to 2
- sketch_cols: bfloat16 [4, 2, 1024, 256], P('seg'), may hold values from -6 to 6
- kept_ranks: int32 [4], P('seg'), may hold values from 128 to 256, as said below
Outputs:
- final_state: bfloat16 [4, 1024, 1024], P('seg', 'sec')
Inputs may be any that keep to these rules, and one draw needn't show every extreme that they name: `kept_ranks`: each segment keeps between 128 and 256 ranks; some segment keeps exactly 256.
All inputs are finite; a program needn't handle non-finite values.
Results may differ from a plain program's by a relative error of at most 0.025.
Values may be sent and summed in bfloat16 or wider, within the bound.
No kernel may reach another device: no remote copies, remote signals or barrier semaphores. Data moves between devices by JAX's collectives and lax.ppermute only.
A program may use at most 128 MiB of HBM per device.

v0:
```python
import jax
import jax.numpy as jnp
from jax import lax
from jax.sharding import PartitionSpec as P

ITERS = 2
TAU = 0.3
MOMENTUM = 0.5
EPS = 1e-06


def from_behind(block, axis, distance):
    devices = range(lax.axis_size(axis))
    route = [(i - distance, i) for i in devices if i - distance in devices]
    return lax.ppermute(block, axis, route)


def left_products(left, rows):
    return jnp.einsum(
        "kij,jn->kin",
        left,
        lax.all_gather(rows, "sec", axis=0, tiled=True),
        preferred_element_type=jnp.float32,
    )


def gradient_step(rows, previous, left, right):
    width = rows.shape[1]
    first = left_products(left, rows).astype(jnp.bfloat16)
    partial_sum = jnp.einsum("kij,kjn->in", first, right, preferred_element_type=jnp.float32)
    total = lax.psum(partial_sum, "mpo")
    shifted = rows.astype(jnp.float32) - TAU * total
    if previous is not None:
        shifted = shifted - MOMENTUM * previous.astype(jnp.float32)
    squares = lax.psum(jnp.sum(shifted * shifted), "sec")
    return (shifted * (width * lax.rsqrt(squares + EPS))).astype(jnp.bfloat16)


def run_steps(start_rows, left, right):
    current = start_rows
    previous = None
    for step in range(ITERS):
        current, previous = (gradient_step(current, previous, left, right), current)
    return current


def truncate(rows, omega, rank):
    columns = omega.shape[1]
    sketch = jnp.dot(rows, omega, preferred_element_type=jnp.float32)
    keep = (jnp.arange(columns) < rank).astype(jnp.float32)
    as_float = rows.astype(jnp.float32)
    gram, cross = lax.psum(
        (
            jnp.dot(sketch.T, sketch, precision=lax.Precision.HIGHEST),
            jnp.dot(sketch.T, as_float, precision=lax.Precision.HIGHEST),
        ),
        "sec",
    )
    factor = jnp.linalg.cholesky(gram)
    basis = (
        lax.linalg.triangular_solve(factor, sketch.T, left_side=True, lower=True).T * keep[None, :]
    )
    coeffs = lax.linalg.triangular_solve(factor, cross, left_side=True, lower=True) * keep[:, None]
    return jnp.dot(basis, coeffs, precision=lax.Precision.HIGHEST).astype(jnp.bfloat16)


def on_device(state, left_env, right_env, inv_singular, sketch_cols, kept_ranks):
    rows = state[0]
    left = left_env[0]
    right = right_env[0]
    scales = inv_singular[0]
    rank = kept_ranks[0]
    width = rows.shape[1]
    neighbour = from_behind(rows, "seg", 1)
    merged = (rows.astype(jnp.float32) + neighbour.astype(jnp.float32) * scales[None, :]).astype(
        jnp.bfloat16
    )
    current = run_steps(merged, left, right)
    middle = truncate(current, sketch_cols[0, 0], rank)
    expanded = left_products(left, middle).astype(jnp.bfloat16)
    summed = lax.psum_scatter(
        jnp.einsum("ia,kin->akn", middle, expanded, preferred_element_type=jnp.float32),
        "sec",
        scatter_dimension=0,
        tiled=True,
    )
    message = (summed * (1.0 / width)).astype(jnp.bfloat16)
    arrived = from_behind(message, "seg", 1)
    left_next = (
        left.astype(jnp.float32) + jnp.transpose(arrived.astype(jnp.float32), (1, 0, 2))
    ).astype(jnp.bfloat16)
    neighbour_two = from_behind(middle, "seg", -1)
    merged_two = (
        middle.astype(jnp.float32) + neighbour_two.astype(jnp.float32) * scales[None, :]
    ).astype(jnp.bfloat16)
    current = run_steps(merged_two, left_next, right)
    final_rows = truncate(current, sketch_cols[0, 1], rank)
    return final_rows[None]


def solution(mesh):
    return jax.shard_map(
        on_device,
        mesh=mesh,
        in_specs=(
            P("seg", "sec", None),
            P("seg", "mpo", "sec", None),
            P("seg", "mpo", None, None),
            P("seg", None),
            P("seg", None, None, None),
            P("seg"),
        ),
        out_specs=P("seg", "sec", None),
        check_vma=False,
    )
```

profile of v0, /device:TPU:0, one launch (start us, length us, event | category | flops | bytes accessed | tf_op | source)
XLA Modules:
  0.0 956.5 jit_solution(16439634779600430897)
XLA Ops:
  6.5 5.0 collective-permute-start
  11.5 22.6 %collective-permute-done = bf16[512,1024]{1,0:T(8,128)(2,1)S(1)} collective-permute-done((bf16[512,1024]{1,0:T(8,128)(2,1)}, bf16[512,1024]{1,0:T(8,128)(2,1)S(1)}, u32[]{:S(2)}, u32[]{:S(2)}) %collective-permute-start) | collective-permute-done | bytes 1048608 | tf_op jit(solution)/shard_map/ppermute | solution.py:15
  34.2 2.7 add_convert_fusion.1
  36.9 35.3 %all-gather.6.cloned.1.call-done = bf16[1024,1024]{1,0:T(8,128)(2,1)} async-done(((bf16[512,1024]{1,0:T(8,128)(2,1)}), bf16[1024,1024]{1,0:T(8,128)(2,1)}) %all-gather.6.cloned.1.call-update) | async-done | bytes 2097168 | tf_op jit(solution)/shard_map/all_gather | solution.py:22
  72.2 5.2 fusion.17
  77.4 7.5 fusion.33
  85.1 51.5 %all-reduce.10.cloned.1.call-done = f32[512,1024]{1,0:T(8,128)} async-done(((f32[512,1024]{1,0:T(8,128)}), f32[512,1024]{1,0:T(8,128)}) %all-reduce.10.cloned.1.call-update) | async-done | bytes 2097168 | tf_op jit(solution)/shard_map/psum | solution.py:31
  136.5 2.9 multiply_reduce_fusion.3
  139.4 5.5 psum.85
  145.7 1.3 multiply_convert_fusion.4
  147.3 33.1 %all-gather.8.cloned.1.call-done = bf16[1024,1024]{1,0:T(8,128)(2,1)} async-done(((bf16[512,1024]{1,0:T(8,128)(2,1)}), bf16[1024,1024]{1,0:T(8,128)(2,1)}) %all-gather.8.cloned.1.call-update) | async-done | bytes 2097168 | tf_op jit(solution)/shard_map/all_gather | solution.py:22
  180.4 5.9 fusion.15
  186.4 7.5 fusion.38
  194.0 51.5 %all-reduce.12.cloned.1.call-done = f32[512,1024]{1,0:T(8,128)} async-done(((f32[512,1024]{1,0:T(8,128)}), f32[512,1024]{1,0:T(8,128)}) %all-reduce.12.cloned.1.call-update) | async-done | bytes 2097168 | tf_op jit(solution)/shard_map/psum | solution.py:31
  245.5 2.8 multiply_reduce_fusion.2
  248.2 5.5 psum.87
  254.5 2.3 multiply_convert_fusion.3
  257.2 2.0 fusion.116
  259.2 1.7 fusion.115
  261.9 45.3 %all-reduce.20.cloned.1.call-done = (f32[256,1024]{1,0:T(8,128)}, f32[256,256]{0,1:T(8,128)}) async-done(((f32[256,1024]{1,0:T(8,128)}, f32[256,256]{0,1:T(8,128)}), (f32[256,1024]{1,0:T(8,128)}, f32[256,256]{0,1:T(8,128)})) %all-reduce.20.cloned.1.call-update) | async-done | bytes 1310736 | tf_op jit(solution)/shard_map/psum | solution.py:52
  307.1 1.1 copy.8
  309.2 11.7 %cholesky.130 = f32[128,128]{1,0:T(8,128)S(1)} custom-call(f32[128,128]{1,0:T(8,128)S(1)} %cholesky.194), custom_call_target="Cholesky" | custom-call | tf_op jit(solution)/shard_map/jit(cholesky)/cholesky | solution.py:59
  321.0 9.8 %custom-call.17 = f32[1,128,128]{1,2,0:T(8,128)S(1)} custom-call(f32[1,128,128]{2,1,0:T(8,128)S(1)} %get-tuple-element.71), custom_call_target="InvertDiagBlocksLowerTriangular" | custom-call | tf_op jit(solution)/shard_map/jit(cholesky)/cholesky | solution.py:59
  331.3 11.7 %cholesky.147 = f32[128,128]{1,0:T(8,128)S(1)} custom-call(f32[128,128]{1,0:T(8,128)S(1)} %convolution_subtract_fusion.5), custom_call_target="Cholesky" | custom-call | tf_op jit(solution)/shard_map/jit(cholesky)/cholesky | solution.py:59
  345.2 4.5 while.8
  346.3 1.4 bitcast_dynamic-update-slice_fusion.4
  348.3 1.4 bitcast_dynamic-update-slice_fusion.4
  349.8 19.7 %custom-call.18 = f32[2,128,128]{1,2,0:T(8,128)S(1)} custom-call(f32[2,128,128]{2,1,0:T(8,128)S(1)} %get-tuple-element.36), custom_call_target="InvertDiagBlocksLowerTriangular" | custom-call | tf_op jit(solution)/shard_map/triangular_solve/custom-call.0 | solution.py:61
  372.8 3.0 convolution_convert_fusion.1
  375.9 33.2 %all-gather.10.cloned.1.call-done = bf16[1024,1024]{1,0:T(8,128)(2,1)} async-done(((bf16[512,1024]{1,0:T(8,128)(2,1)}), bf16[1024,1024]{1,0:T(8,128)(2,1)}) %all-gather.10.cloned.1.call-update) | async-done | bytes 2097168 | tf_op jit(solution)/shard_map/all_gather | solution.py:22
  409.1 11.1 %fusion.9 = f32[1024,3,1024]{2,0,1:T(8,128)} fusion(bf16[1,3,512,1024]{3,2,1,0:T(8,128)(2,1)S(1)} %copy-done.11, bf16[1024,1024]{1,0:T(8,128)(2,1)} %all-gather.10.cloned.1.call-done, bf16[512,1024]{1,0:T(8,128)(2,1)} %convolution_convert_fusion.1), kind=kOutput, calls=%fused_computation.15 | convolution fusion | flops 6444023808 | bytes 18874368 | tf_op jit(solution)/shard_map/ia,kin->akn/dot_general | solution.py:82
  420.3 1.1 copy-done.4
  421.4 1.3 collective-permute-start.1
  422.7 142.1 %reduce-scatter.2.cloned.1.call-done = f32[512,3,1024]{2,0,1:T(8,128)} async-done(((f32[1024,3,1024]{2,0,1:T(8,128)}), f32[512,3,1024]{2,0,1:T(8,128)}) %reduce-scatter.2.cloned.1.call-update) | async-done | bytes 6291472 | tf_op jit(solution)/shard_map/reduce_scatter | solution.py:81
  564.8 5.4 multiply_convert_fusion
  570.2 5.1 collective-permute-start.2
  575.3 1.4 add_convert_fusion
  576.9 30.5 %all-gather.12.cloned.1.call-done = bf16[1024,1024]{1,0:T(8,128)(2,1)} async-done(((bf16[512,1024]{1,0:T(8,128)(2,1)}), bf16[1024,1024]{1,0:T(8,128)(2,1)}) %all-gather.12.cloned.1.call-update) | async-done | bytes 2097168 | tf_op jit(solution)/shard_map/all_gather | solution.py:22
  607.4 33.9 %collective-permute-done.2 = bf16[512,3,1024]{2,0,1:T(8,128)(2,1)} collective-permute-done((bf16[512,3,1024]{2,0,1:T(8,128)(2,1)}, bf16[512,3,1024]{2,0,1:T(8,128)(2,1)}, u32[]{:S(2)}, u32[]{:S(2)}) %collective-permute-start.2) | collective-permute-done | bytes 3145760 | tf_op jit(solution)/shard_map/ppermute | solution.py:15
  641.3 6.9 fusion.28
  648.2 7.6 fusion.43
  655.9 52.5 %all-reduce.14.cloned.1.call-done = f32[512,1024]{1,0:T(8,128)} async-done(((f32[512,1024]{1,0:T(8,128)}), f32[512,1024]{1,0:T(8,128)}) %all-reduce.14.cloned.1.call-update) | async-done | bytes 2097168 | tf_op jit(solution)/shard_map/psum | solution.py:31
  708.4 2.9 multiply_reduce_fusion.1
  711.3 5.5 psum.91
  717.5 1.3 multiply_convert_fusion.2
  718.9 33.3 %all-gather.14.cloned.1.call-done = bf16[1024,1024]{1,0:T(8,128)(2,1)} async-done(((bf16[512,1024]{1,0:T(8,128)(2,1)}), bf16[1024,1024]{1,0:T(8,128)(2,1)}) %all-gather.14.cloned.1.call-update) | async-done | bytes 2097168 | tf_op jit(solution)/shard_map/all_gather | solution.py:22
  752.3 6.9 fusion.26
  759.2 7.5 fusion.48
  766.8 51.5 %all-reduce.16.cloned.1.call-done = f32[512,1024]{1,0:T(8,128)} async-done(((f32[512,1024]{1,0:T(8,128)}), f32[512,1024]{1,0:T(8,128)}) %all-reduce.16.cloned.1.call-update) | async-done | bytes 2097168 | tf_op jit(solution)/shard_map/psum | solution.py:31
  818.3 2.8 multiply_reduce_fusion
  821.0 5.8 psum.93
  827.5 2.3 multiply_convert_fusion.1
  830.2 2.0 fusion.118
  832.2 1.7 fusion.117
  834.0 46.2 %all-reduce.18.cloned.1.call-done = (f32[256,1024]{1,0:T(8,128)}, f32[256,256]{0,1:T(8,128)}) async-done(((f32[256,1024]{1,0:T(8,128)}, f32[256,256]{0,1:T(8,128)}), (f32[256,1024]{1,0:T(8,128)}, f32[256,256]{0,1:T(8,128)})) %all-reduce.18.cloned.1.call-update) | async-done | bytes 1310736 | tf_op jit(solution)/shard_map/psum | solution.py:52
  880.2 1.1 copy.11
  882.2 11.7 %cholesky.164 = f32[128,128]{1,0:T(8,128)S(1)} custom-call(f32[128,128]{1,0:T(8,128)S(1)} %cholesky.197), custom_call_target="Cholesky" | custom-call | tf_op jit(solution)/shard_map/jit(cholesky)/cholesky | solution.py:59
  894.0 9.8 %custom-call.20 = f32[1,128,128]{1,2,0:T(8,128)S(1)} custom-call(f32[1,128,128]{2,1,0:T(8,128)S(1)} %get-tuple-element.67), custom_call_target="InvertDiagBlocksLowerTriangular" | custom-call | tf_op jit(solution)/shard_map/jit(cholesky)/cholesky | solution.py:59
  904.3 11.9 %cholesky.181 = f32[128,128]{1,0:T(8,128)S(1)} custom-call(f32[128,128]{1,0:T(8,128)S(1)} %convolution_subtract_fusion.4), custom_call_target="Cholesky" | custom-call | tf_op jit(solution)/shard_map/jit(cholesky)/cholesky | solution.py:59
  919.0 4.1 while.9
  919.7 1.4 bitcast_dynamic-update-slice_fusion.5
  921.7 1.4 bitcast_dynamic-update-slice_fusion.5
  923.2 19.7 %custom-call.21 = f32[2,128,128]{1,2,0:T(8,128)S(1)} custom-call(f32[2,128,128]{2,1,0:T(8,128)S(1)} %get-tuple-element.38), custom_call_target="InvertDiagBlocksLowerTriangular" | custom-call | tf_op jit(solution)/shard_map/triangular_solve/custom-call.0 | solution.py:61
  946.2 3.0 fusion.53
  (98 shorter events, 16.5 us)
Async XLA Ops:
  6.5 65.7 %all-gather.6.cloned.1.call-start = ((), (), s32[]{:S(2)}) async-start(), calls=%async_computation.1 | async-start | bytes 3145728 | tf_op jit(solution)/shard_map/all_gather | solution.py:22
  6.5 27.6 %collective-permute-start = (bf16[512,1024]{1,0:T(8,128)(2,1)}, bf16[512,1024]{1,0:T(8,128)(2,1)S(1)}, u32[]{:S(2)}, u32[]{:S(2)}) collective-permute-start(bf16[512,1024]{1,0:T(8,128)(2,1)} %bitcast.191), channel_id=1, source_target_pairs={{0,8},{8,16},{16,24},{1,9},{9,17},{17,25},{2,10},{10,18},{18,26},{... | collective-permute-start | bytes 3145736 | tf_op jit(solution)/shard_map/ppermute | solution.py:15
  34.2 38.0 %copy-start.10 = (bf16[1,3,512,1024]{3,2,1,0:T(8,128)(2,1)S(1)}, bf16[1,3,512,1024]{3,2,1,0:T(8,128)(2,1)}, u32[]{:S(2)}) copy-start(bf16[1,3,512,1024]{3,2,1,0:T(8,128)(2,1)} %param.12) | copy-start | bytes 9437188
  36.9 99.6 %all-reduce.10.cloned.1.call-start = ((), (), s32[]{:S(2)}) async-start(), calls=%async_computation.2 | async-start | bytes 4194304 | tf_op jit(solution)/shard_map/psum | solution.py:31
  85.0 51.6 %copy-start.1 = (bf16[512,1024]{1,0:T(8,128)(2,1)S(1)}, bf16[512,1024]{1,0:T(8,128)(2,1)}, u32[]{:S(2)}) copy-start(bf16[512,1024]{1,0:T(8,128)(2,1)} %add_convert_fusion.1) | copy-start | bytes 3145732
  85.0 95.4 %all-gather.8.cloned.1.call-start = ((), (), s32[]{:S(2)}) async-start(), calls=%async_computation.3 | async-start | bytes 3145728 | tf_op jit(solution)/shard_map/all_gather | solution.py:22
  136.5 9.1 copy-start.5
  147.1 98.4 %all-reduce.12.cloned.1.call-start = ((), (), s32[]{:S(2)}) async-start(), calls=%async_computation.4 | async-start | bytes 4194304 | tf_op jit(solution)/shard_map/psum | solution.py:31
  193.9 51.6 %copy-start.3 = (bf16[512,1024]{1,0:T(8,128)(2,1)S(1)}, bf16[512,1024]{1,0:T(8,128)(2,1)}, u32[]{:S(2)}) copy-start(bf16[512,1024]{1,0:T(8,128)(2,1)} %multiply_convert_fusion.4) | copy-start | bytes 3145732
  193.9 113.2 %all-reduce.20.cloned.1.call-start = ((), (), s32[]{:S(2)}) async-start(), calls=%async_computation.12 | async-start | bytes 2621440 | tf_op jit(solution)/shard_map/psum | solution.py:52
  254.5 2.3 copy-start.12
  261.0 148.1 %all-gather.10.cloned.1.call-start = ((), (), s32[]{:S(2)}) async-start(), calls=%async_computation.5 | async-start | bytes 3145728 | tf_op jit(solution)/shard_map/all_gather | solution.py:22
  330.8 40.1 %copy-start.7 = (f32[256,1024]{1,0:T(8,128)S(1)}, f32[256,1024]{1,0:T(8,128)}, u32[]{:S(2)}) copy-start(f32[256,1024]{1,0:T(8,128)} %get-tuple-element.58) | copy-start | bytes 3145732
  372.8 36.3 %copy-start.11 = (bf16[1,3,512,1024]{3,2,1,0:T(8,128)(2,1)S(1)}, bf16[1,3,512,1024]{3,2,1,0:T(8,128)(2,1)}, u32[]{:S(2)}) copy-start(bf16[1,3,512,1024]{3,2,1,0:T(8,128)(2,1)} %param.12) | copy-start | bytes 9437188
  375.8 189.0 %reduce-scatter.2.cloned.1.call-start = ((), (), s32[]{:S(2)}) async-start(), calls=%async_computation.6 | async-start | bytes 18874368 | tf_op jit(solution)/shard_map/reduce_scatter | solution.py:81
  420.2 1.2 copy-start.4
  420.2 155.1 %copy-start.9 = (f32[1,1024]{1,0:T(1,128)S(1)}, f32[1,1024]{1,0:T(1,128)}, u32[]{:S(2)}) copy-start(f32[1,1024]{1,0:T(1,128)} %param.14) | copy-start | bytes 12292
  420.2 187.2 %all-gather.12.cloned.1.call-start = ((), (), s32[]{:S(2)}) async-start(), calls=%async_computation.7 | async-start | bytes 3145728 | tf_op jit(solution)/shard_map/all_gather | solution.py:22
  421.4 153.9 %collective-permute-start.1 = (bf16[512,1024]{1,0:T(8,128)(2,1)S(1)}, bf16[512,1024]{1,0:T(8,128)(2,1)S(1)}, u32[]{:S(2)}, u32[]{:S(2)}) collective-permute-start(bf16[512,1024]{1,0:T(8,128)(2,1)S(1)} %copy-done.4), channel_id=1, source_target_pairs={{8,0},{16,8},{24,16},{9,1},{17,9},{25,17},{10,2},{18,10},{26,18},{... | collective-permute-start | bytes 3145736 | tf_op jit(solution)/shard_map/ppermute | solution.py:15
  570.2 71.0 %collective-permute-start.2 = (bf16[512,3,1024]{2,0,1:T(8,128)(2,1)}, bf16[512,3,1024]{2,0,1:T(8,128)(2,1)}, u32[]{:S(2)}, u32[]{:S(2)}) collective-permute-start(bf16[512,3,1024]{2,0,1:T(8,128)(2,1)} %multiply_convert_fusion), channel_id=1, source_target_pairs={{0,8},{8,16},{16,24},{1,9},{9,17},{17,25},{2,10},{10,18},{18,26},{... | collective-permute-start | bytes 9437192 | tf_op jit(solution)/shard_map/ppermute | solution.py:15
  576.7 131.7 %all-reduce.14.cloned.1.call-start = ((), (), s32[]{:S(2)}) async-start(), calls=%async_computation.8 | async-start | bytes 4194304 | tf_op jit(solution)/shard_map/psum | solution.py:31
  655.8 52.6 %copy-start = (bf16[512,1024]{1,0:T(8,128)(2,1)S(1)}, bf16[512,1024]{1,0:T(8,128)(2,1)}, u32[]{:S(2)}) copy-start(bf16[512,1024]{1,0:T(8,128)(2,1)} %add_convert_fusion) | copy-start | bytes 3145732
  655.8 96.4 %all-gather.14.cloned.1.call-start = ((), (), s32[]{:S(2)}) async-start(), calls=%async_computation.9 | async-start | bytes 3145728 | tf_op jit(solution)/shard_map/all_gather | solution.py:22
  708.4 9.1 copy-start.6
  718.9 99.4 %all-reduce.16.cloned.1.call-start = ((), (), s32[]{:S(2)}) async-start(), calls=%async_computation.10 | async-start | bytes 4194304 | tf_op jit(solution)/shard_map/psum | solution.py:31
  766.7 51.6 %copy-start.2 = (bf16[512,1024]{1,0:T(8,128)(2,1)S(1)}, bf16[512,1024]{1,0:T(8,128)(2,1)}, u32[]{:S(2)}) copy-start(bf16[512,1024]{1,0:T(8,128)(2,1)} %multiply_convert_fusion.2) | copy-start | bytes 3145732
  766.7 113.4 %all-reduce.18.cloned.1.call-start = ((), (), s32[]{:S(2)}) async-start(), calls=%async_computation.11 | async-start | bytes 2621440 | tf_op jit(solution)/shard_map/psum | solution.py:52
  827.5 2.3 copy-start.13
  903.8 40.5 %copy-start.8 = (f32[256,1024]{1,0:T(8,128)S(1)}, f32[256,1024]{1,0:T(8,128)}, u32[]{:S(2)}) copy-start(f32[256,1024]{1,0:T(8,128)} %get-tuple-element.56) | copy-start | bytes 3145732
Sparse Core Ops, SparseCore 0:
  37.0 35.1 all-gather.5
  85.1 51.3 all-reduce.9
  147.2 33.1 all-gather.7
  194.0 51.3 all-reduce.11
  261.1 46.0 all-reduce.19
  375.9 33.0 all-gather.9
  420.3 144.4 reduce-scatter.1
  576.8 30.5 all-gather.11
  655.9 52.3 all-reduce.13
  719.0 33.1 all-gather.13
  766.8 51.3 all-reduce.15
  834.1 46.0 all-reduce.17
where the time goes:
time: 962 us; the launch traced here: 956 us
  waiting for transfers between devices  663 us (69%)
  other arithmetic  138 us (14%)
  matrix products  88.1 us (9%)
  blocking collectives  22.4 us (2%)
  between operations  20.6 us (2%)
  starting transfers between devices  12.3 us (1%)
  local copies, waits for them, and re-layouts  11.6 us (1%)
    psum x4, waiting for transfers between devices, gradient_step(): total = lax.psum(partial_sum, 'mpo')  207 us
    all_gather x5, waiting for transfers between devices, left_products(): lax.all_gather(rows, 'sec', axis=0, tiled=True)  165 us
    reduce_scatter x1, waiting for transfers between devices, on_device(): lax.psum_scatter(jnp.einsum('ia,kin->akn', middle, expanded, preferred_el...  142 us
    psum x2, waiting for transfers between devices, truncate(): lax.psum((jnp.dot(sketch.T, sketch, precision=lax.Precision.HIGHEST), jnp...  91.4 us
    another operation x13, other arithmetic, truncate(): factor = jnp.linalg.cholesky(gram)  68.9 us
    ppermute x3, waiting for transfers between devices, from_behind(): return lax.ppermute(block, axis, route)  56.5 us
    another operation x5, other arithmetic, truncate(): lax.linalg.triangular_solve(factor, sketch.T, left_side=True, lower=True)  39.4 us
    dot_general x4, matrix products, gradient_step(): jnp.einsum('kij,kjn->in', first, right, preferred_element_type=jnp.float32)  30.2 us
  transfers between devices with their start and end apart: 15, of which 14 were waited for; matrix products, arithmetic and copies ran while one was open for 1% of the time, Pallas kernels for 0%

commit v1 on v0

--- a/solution.py
+++ b/solution.py
@@ -1,3 +1,4 @@
+import functools
 import jax
 import jax.numpy as jnp
 from jax import lax
@@ -7,6 +8,14 @@
 TAU = 0.3
 MOMENTUM = 0.5
 EPS = 1e-06
+
+
+def balance_the_pairs_all(block_here, axis_name):
+    block_out = jax.lax.all_gather(block_here, axis_name)
+    return jnp.sum(block_out, 0)
+
+
+clusters_number = functools.partial(balance_the_pairs_all, axis_name="mpo")
 
 
 def from_behind(block, axis, distance):
@@ -28,7 +37,7 @@
     width = rows.shape[1]
     first = left_products(left, rows).astype(jnp.bfloat16)
     partial_sum = jnp.einsum("kij,kjn->in", first, right, preferred_element_type=jnp.float32)
-    total = lax.psum(partial_sum, "mpo")
+    total = clusters_number(partial_sum)
     shifted = rows.astype(jnp.float32) - TAU * total
     if previous is not None:
         shifted = shifted - MOMENTUM * previous.astype(jnp.float32)

time: 962 us -> 1000 us (1.040)
  waiting for transfers between devices: 663 us -> 690 us
  other arithmetic: 138 us -> 152 us
    all_gather x0 -> x4, waiting for transfers between devices: none -> 235 us  [balance_the_pairs_all(): block_out = jax.lax.all_gather(block_here, axis_name)]
    psum x4 -> x0, waiting for transfers between devices: 207 us -> none  [gradient_step(): total = lax.psum(partial_sum, 'mpo')]
    reduce_sum x0 -> x4, other arithmetic: none -> 18.4 us  [balance_the_pairs_all(): return jnp.sum(block_out, 0)]
where the time goes in v1:
time: 1000 us; the launch traced here: 998 us
  waiting for transfers between devices  690 us (69%)
  other arithmetic  152 us (15%)
  matrix products  88.4 us (9%)
  blocking collectives  22.6 us (2%)
  between operations  20.7 us (2%)
  starting transfers between devices  12.4 us (1%)
  local copies, waits for them, and re-layouts  11.6 us (1%)
    all_gather x4, waiting for transfers between devices, balance_the_pairs_all(): block_out = jax.lax.all_gather(block_here, axis_name)  235 us
    all_gather x5, waiting for transfers between devices, left_products(): lax.all_gather(rows, 'sec', axis=0, tiled=True)  165 us
    reduce_scatter x1, waiting for transfers between devices, on_device(): lax.psum_scatter(jnp.einsum('ia,kin->akn', middle, expanded, preferred_el...  142 us
    psum x2, waiting for transfers between devices, truncate(): lax.psum((jnp.dot(sketch.T, sketch, precision=lax.Precision.HIGHEST), jnp...  91.3 us
    another operation x13, other arithmetic, truncate(): factor = jnp.linalg.cholesky(gram)  68.9 us
    ppermute x3, waiting for transfers between devices, from_behind(): return lax.ppermute(block, axis, route)  56.5 us
    another operation x5, other arithmetic, truncate(): lax.linalg.triangular_solve(factor, sketch.T, left_side=True, lower=True)  39.4 us
    dot_general x4, matrix products, gradient_step(): jnp.einsum('kij,kjn->in', first, right, preferred_element_type=jnp.float32)  30.6 us
  transfers between devices with their start and end apart: 15, of which 14 were waited for; matrix products, arithmetic and copies ran while one was open for 1% of the time, Pallas kernels for 0%

profile of v1, /device:TPU:0, one launch (start us, length us, event | category | flops | bytes accessed | tf_op | source)
XLA Modules:
  0.0 998.0 jit_solution(5652541454124897087)
XLA Ops:
  6.5 5.0 collective-permute-start
  11.5 22.6 %collective-permute-done = bf16[512,1024]{1,0:T(8,128)(2,1)S(1)} collective-permute-done((bf16[512,1024]{1,0:T(8,128)(2,1)}, bf16[512,1024]{1,0:T(8,128)(2,1)S(1)}, u32[]{:S(2)}, u32[]{:S(2)}) %collective-permute-start) | collective-permute-done | bytes 1048608 | tf_op jit(solution)/shard_map/ppermute | solution.py:24
  34.2 2.7 add_convert_fusion.1
  36.9 35.3 %all-gather.14.cloned.1.call-done = bf16[1024,1024]{1,0:T(8,128)(2,1)} async-done(((bf16[512,1024]{1,0:T(8,128)(2,1)}), bf16[1024,1024]{1,0:T(8,128)(2,1)}) %all-gather.14.cloned.1.call-update) | async-done | bytes 2097168 | tf_op jit(solution)/shard_map/all_gather | solution.py:31
  72.2 5.2 fusion.17
  77.4 7.6 fusion.33
  85.1 58.4 %all-gather.24.cloned.1.call-done = f32[2048,1024]{1,0:T(8,128)} async-done(((f32[512,1024]{1,0:T(8,128)}), f32[2048,1024]{1,0:T(8,128)}) %all-gather.24.cloned.1.call-update) | async-done | bytes 8388624 | tf_op jit(solution)/shard_map/all_gather | solution.py:14
  143.5 4.6 reduce_sum.72
  148.2 1.2 multiply_reduce_fusion.3
  149.4 5.5 psum.56
  155.6 1.3 multiply_convert_fusion.4
  157.2 33.1 %all-gather.16.cloned.1.call-done = bf16[1024,1024]{1,0:T(8,128)(2,1)} async-done(((bf16[512,1024]{1,0:T(8,128)(2,1)}), bf16[1024,1024]{1,0:T(8,128)(2,1)}) %all-gather.16.cloned.1.call-update) | async-done | bytes 2097168 | tf_op jit(solution)/shard_map/all_gather | solution.py:31
  190.3 5.9 fusion.15
  196.2 7.6 fusion.38
  203.9 58.4 %all-gather.26.cloned.1.call-done = f32[2048,1024]{1,0:T(8,128)} async-done(((f32[512,1024]{1,0:T(8,128)}), f32[2048,1024]{1,0:T(8,128)}) %all-gather.26.cloned.1.call-update) | async-done | bytes 8388624 | tf_op jit(solution)/shard_map/all_gather | solution.py:14
  262.3 4.6 reduce_sum.74
  266.9 2.5 multiply_reduce_fusion.2
  269.3 5.6 psum.57
  275.7 1.9 multiply_convert_fusion.3
  278.1 2.0 fusion.116
  280.1 1.7 fusion.115
  282.8 45.2 %all-reduce.8.cloned.1.call-done = (f32[256,1024]{1,0:T(8,128)}, f32[256,256]{0,1:T(8,128)}) async-done(((f32[256,1024]{1,0:T(8,128)}, f32[256,256]{0,1:T(8,128)}), (f32[256,1024]{1,0:T(8,128)}, f32[256,256]{0,1:T(8,128)})) %all-reduce.8.cloned.1.call-update) | async-done | bytes 1310736 | tf_op jit(solution)/shard_map/psum | solution.py:61
  330.0 11.7 %cholesky.130 = f32[128,128]{1,0:T(8,128)S(1)} custom-call(f32[128,128]{1,0:T(8,128)S(1)} %cholesky.194), custom_call_target="Cholesky" | custom-call | tf_op jit(solution)/shard_map/jit(cholesky)/cholesky | solution.py:68
  341.8 9.8 custom-call.17
  352.1 11.7 %cholesky.147 = f32[128,128]{1,0:T(8,128)S(1)} custom-call(f32[128,128]{1,0:T(8,128)S(1)} %convolution_subtract_fusion.5), custom_call_target="Cholesky" | custom-call | tf_op jit(solution)/shard_map/jit(cholesky)/cholesky | solution.py:68
  366.0 4.6 while.8
  367.1 1.4 bitcast_dynamic-update-slice_fusion.4
  369.2 1.4 bitcast_dynamic-update-slice_fusion.4
  370.6 19.7 %custom-call.18 = f32[2,128,128]{1,2,0:T(8,128)S(1)} custom-call(f32[2,128,128]{2,1,0:T(8,128)S(1)} %get-tuple-element.36), custom_call_target="InvertDiagBlocksLowerTriangular" | custom-call | tf_op jit(solution)/shard_map/triangular_solve/custom-call.0 | solution.py:70
  393.6 3.0 convolution_convert_fusion.1
  396.7 33.2 %all-gather.18.cloned.1.call-done = bf16[1024,1024]{1,0:T(8,128)(2,1)} async-done(((bf16[512,1024]{1,0:T(8,128)(2,1)}), bf16[1024,1024]{1,0:T(8,128)(2,1)}) %all-gather.18.cloned.1.call-update) | async-done | bytes 2097168 | tf_op jit(solution)/shard_map/all_gather | solution.py:31
  429.9 11.1 %fusion.9 = f32[1024,3,1024]{2,0,1:T(8,128)} fusion(bf16[1,3,512,1024]{3,2,1,0:T(8,128)(2,1)S(1)} %copy-done.7, bf16[1024,1024]{1,0:T(8,128)(2,1)} %all-gather.18.cloned.1.call-done, bf16[512,1024]{1,0:T(8,128)(2,1)} %convolution_convert_fusion.1), kind=kOutput, calls=%fused_computation.15 | convolution fusion | flops 6444023808 | bytes 18874368 | tf_op jit(solution)/shard_map/ia,kin->akn/dot_general | solution.py:91
  442.3 1.3 collective-permute-start.1
  443.6 142.1 %reduce-scatter.2.cloned.1.call-done = f32[512,3,1024]{2,0,1:T(8,128)} async-done(((f32[1024,3,1024]{2,0,1:T(8,128)}), f32[512,3,1024]{2,0,1:T(8,128)}) %reduce-scatter.2.cloned.1.call-update) | async-done | bytes 6291472 | tf_op jit(solution)/shard_map/reduce_scatter | solution.py:90
  585.7 5.4 multiply_convert_fusion
  591.1 5.1 collective-permute-start.2
  596.2 1.4 add_convert_fusion
  597.8 30.4 %all-gather.20.cloned.1.call-done = bf16[1024,1024]{1,0:T(8,128)(2,1)} async-done(((bf16[512,1024]{1,0:T(8,128)(2,1)}), bf16[1024,1024]{1,0:T(8,128)(2,1)}) %all-gather.20.cloned.1.call-update) | async-done | bytes 2097168 | tf_op jit(solution)/shard_map/all_gather | solution.py:31
  628.2 33.9 %collective-permute-done.2 = bf16[512,3,1024]{2,0,1:T(8,128)(2,1)} collective-permute-done((bf16[512,3,1024]{2,0,1:T(8,128)(2,1)}, bf16[512,3,1024]{2,0,1:T(8,128)(2,1)}, u32[]{:S(2)}, u32[]{:S(2)}) %collective-permute-start.2) | collective-permute-done | bytes 3145760 | tf_op jit(solution)/shard_map/ppermute | solution.py:24
  662.1 6.9 fusion.28
  669.0 7.7 fusion.43
  676.7 59.4 %all-gather.28.cloned.1.call-done = f32[2048,1024]{1,0:T(8,128)} async-done(((f32[512,1024]{1,0:T(8,128)}), f32[2048,1024]{1,0:T(8,128)}) %all-gather.28.cloned.1.call-update) | async-done | bytes 8388624 | tf_op jit(solution)/shard_map/all_gather | solution.py:14
  736.1 4.6 reduce_sum.76
  742.0 5.5 psum.60
  748.2 1.3 multiply_convert_fusion.2
  749.6 33.2 %all-gather.22.cloned.1.call-done = bf16[1024,1024]{1,0:T(8,128)(2,1)} async-done(((bf16[512,1024]{1,0:T(8,128)(2,1)}), bf16[1024,1024]{1,0:T(8,128)(2,1)}) %all-gather.22.cloned.1.call-update) | async-done | bytes 2097168 | tf_op jit(solution)/shard_map/all_gather | solution.py:31
  782.9 6.9 fusion.26
  789.8 7.6 fusion.48
  797.5 58.4 %all-gather.30.cloned.1.call-done = f32[2048,1024]{1,0:T(8,128)} async-done(((f32[512,1024]{1,0:T(8,128)}), f32[2048,1024]{1,0:T(8,128)}) %all-gather.30.cloned.1.call-update) | async-done | bytes 8388624 | tf_op jit(solution)/shard_map/all_gather | solution.py:14
  855.9 4.6 reduce_sum.78
  860.4 2.5 multiply_reduce_fusion
  862.9 5.8 psum.61
  869.5 1.9 multiply_convert_fusion.1
  871.8 2.0 fusion.118
  873.8 1.7 fusion.117
  875.6 46.1 %all-reduce.6.cloned.1.call-done = (f32[256,1024]{1,0:T(8,128)}, f32[256,256]{0,1:T(8,128)}) async-done(((f32[256,1024]{1,0:T(8,128)}, f32[256,256]{0,1:T(8,128)}), (f32[256,1024]{1,0:T(8,128)}, f32[256,256]{0,1:T(8,128)})) %all-reduce.6.cloned.1.call-update) | async-done | bytes 1310736 | tf_op jit(solution)/shard_map/psum | solution.py:61
  923.8 11.7 %cholesky.164 = f32[128,128]{1,0:T(8,128)S(1)} custom-call(f32[128,128]{1,0:T(8,128)S(1)} %cholesky.197), custom_call_target="Cholesky" | custom-call | tf_op jit(solution)/shard_map/jit(cholesky)/cholesky | solution.py:68
  935.5 9.8 custom-call.20
  945.8 11.9 %cholesky.181 = f32[128,128]{1,0:T(8,128)S(1)} custom-call(f32[128,128]{1,0:T(8,128)S(1)} %convolution_subtract_fusion.4), custom_call_target="Cholesky" | custom-call | tf_op jit(solution)/shard_map/jit(cholesky)/cholesky | solution.py:68
  960.6 4.1 while.9
  961.2 1.4 bitcast_dynamic-update-slice_fusion.5
  963.2 1.4 bitcast_dynamic-update-slice_fusion.5
  964.7 19.7 %custom-call.21 = f32[2,128,128]{1,2,0:T(8,128)S(1)} custom-call(f32[2,128,128]{2,1,0:T(8,128)S(1)} %get-tuple-element.38), custom_call_target="InvertDiagBlocksLowerTriangular" | custom-call | tf_op jit(solution)/shard_map/triangular_solve/custom-call.0 | solution.py:70
  987.7 3.0 fusion.53
  (94 shorter events, 20.9 us)
Async XLA Ops:
  6.5 65.7 %all-gather.14.cloned.1.call-start = ((), (), s32[]{:S(2)}) async-start(), calls=%async_computation.1 | async-start | bytes 3145728 | tf_op jit(solution)/shard_map/all_gather | solution.py:31
  6.5 27.6 %collective-permute-start = (bf16[512,1024]{1,0:T(8,128)(2,1)}, bf16[512,1024]{1,0:T(8,128)(2,1)S(1)}, u32[]{:S(2)}, u32[]{:S(2)}) collective-permute-start(bf16[512,1024]{1,0:T(8,128)(2,1)} %bitcast.199), channel_id=1, source_target_pairs={{0,8},{8,16},{16,24},{1,9},{9,17},{17,25},{2,10},{10,18},{18,26},{... | collective-permute-start | bytes 3145736 | tf_op jit(solution)/shard_map/ppermute | solution.py:24
  34.2 38.0 %copy-start.6 = (bf16[1,3,512,1024]{3,2,1,0:T(8,128)(2,1)S(1)}, bf16[1,3,512,1024]{3,2,1,0:T(8,128)(2,1)}, u32[]{:S(2)}) copy-start(bf16[1,3,512,1024]{3,2,1,0:T(8,128)(2,1)} %param.12) | copy-start | bytes 9437188
  36.9 106.6 %all-gather.24.cloned.1.call-start = ((), (), s32[]{:S(2)}) async-start(), calls=%async_computation.7 | async-start | bytes 10485760 | tf_op jit(solution)/shard_map/all_gather | solution.py:14
  85.1 105.2 %all-gather.16.cloned.1.call-start = ((), (), s32[]{:S(2)}) async-start(), calls=%async_computation.2 | async-start | bytes 3145728 | tf_op jit(solution)/shard_map/all_gather | solution.py:31
  143.5 4.6 copy-start.1
  157.0 105.3 %all-gather.26.cloned.1.call-start = ((), (), s32[]{:S(2)}) async-start(), calls=%async_computation.8 | async-start | bytes 10485760 | tf_op jit(solution)/shard_map/all_gather | solution.py:14
  203.9 124.1 %all-reduce.8.cloned.1.call-start = ((), (), s32[]{:S(2)}) async-start(), calls=%async_computation.12 | async-start | bytes 2621440 | tf_op jit(solution)/shard_map/psum | solution.py:61
  275.7 1.9 copy-start.8
  281.8 148.1 %all-gather.18.cloned.1.call-start = ((), (), s32[]{:S(2)}) async-start(), calls=%async_computation.3 | async-start | bytes 3145728 | tf_op jit(solution)/shard_map/all_gather | solution.py:31
  351.6 40.1 %copy-start.3 = (f32[256,1024]{1,0:T(8,128)S(1)}, f32[256,1024]{1,0:T(8,128)}, u32[]{:S(2)}) copy-start(f32[256,1024]{1,0:T(8,128)} %get-tuple-element.58) | copy-start | bytes 3145732
  393.6 36.3 %copy-start.7 = (bf16[1,3,512,1024]{3,2,1,0:T(8,128)(2,1)S(1)}, bf16[1,3,512,1024]{3,2,1,0:T(8,128)(2,1)}, u32[]{:S(2)}) copy-start(bf16[1,3,512,1024]{3,2,1,0:T(8,128)(2,1)} %param.12) | copy-start | bytes 9437188
  396.7 189.0 %reduce-scatter.2.cloned.1.call-start = ((), (), s32[]{:S(2)}) async-start(), calls=%async_computation.4 | async-start | bytes 18874368 | tf_op jit(solution)/shard_map/reduce_scatter | solution.py:90
  441.0 1.2 copy-start.2
  441.1 155.1 %copy-start.5 = (f32[1,1024]{1,0:T(1,128)S(1)}, f32[1,1024]{1,0:T(1,128)}, u32[]{:S(2)}) copy-start(f32[1,1024]{1,0:T(1,128)} %param.14) | copy-start | bytes 12292
  441.1 187.1 %all-gather.20.cloned.1.call-start = ((), (), s32[]{:S(2)}) async-start(), calls=%async_computation.5 | async-start | bytes 3145728 | tf_op jit(solution)/shard_map/all_gather | solution.py:31
  442.3 153.9 %collective-permute-start.1 = (bf16[512,1024]{1,0:T(8,128)(2,1)S(1)}, bf16[512,1024]{1,0:T(8,128)(2,1)S(1)}, u32[]{:S(2)}, u32[]{:S(2)}) collective-permute-start(bf16[512,1024]{1,0:T(8,128)(2,1)S(1)} %copy-done.2), channel_id=1, source_target_pairs={{8,0},{16,8},{24,16},{9,1},{17,9},{25,17},{10,2},{18,10},{26,18},{... | collective-permute-start | bytes 3145736 | tf_op jit(solution)/shard_map/ppermute | solution.py:24
  591.1 71.0 %collective-permute-start.2 = (bf16[512,3,1024]{2,0,1:T(8,128)(2,1)}, bf16[512,3,1024]{2,0,1:T(8,128)(2,1)}, u32[]{:S(2)}, u32[]{:S(2)}) collective-permute-start(bf16[512,3,1024]{2,0,1:T(8,128)(2,1)} %multiply_convert_fusion), channel_id=1, source_target_pairs={{0,8},{8,16},{16,24},{1,9},{9,17},{17,25},{2,10},{10,18},{18,26},{... | collective-permute-start | bytes 9437192 | tf_op jit(solution)/shard_map/ppermute | solution.py:24
  597.6 138.5 %all-gather.28.cloned.1.call-start = ((), (), s32[]{:S(2)}) async-start(), calls=%async_computation.9 | async-start | bytes 10485760 | tf_op jit(solution)/shard_map/all_gather | solution.py:14
  676.7 106.2 %all-gather.22.cloned.1.call-start = ((), (), s32[]{:S(2)}) async-start(), calls=%async_computation.6 | async-start | bytes 3145728 | tf_op jit(solution)/shard_map/all_gather | solution.py:31
  736.1 4.6 copy-start
  749.6 106.3 %all-gather.30.cloned.1.call-start = ((), (), s32[]{:S(2)}) async-start(), calls=%async_computation.10 | async-start | bytes 10485760 | tf_op jit(solution)/shard_map/all_gather | solution.py:14
  797.4 124.3 %all-reduce.6.cloned.1.call-start = ((), (), s32[]{:S(2)}) async-start(), calls=%async_computation.11 | async-start | bytes 2621440 | tf_op jit(solution)/shard_map/psum | solution.py:61
  869.5 1.9 copy-start.9
  945.4 40.5 %copy-start.4 = (f32[256,1024]{1,0:T(8,128)S(1)}, f32[256,1024]{1,0:T(8,128)}, u32[]{:S(2)}) copy-start(f32[256,1024]{1,0:T(8,128)} %get-tuple-element.56) | copy-start | bytes 3145732
Sparse Core Ops, SparseCore 0:
  37.0 35.1 all-gather.13
  85.2 58.2 all-gather.23
  157.1 33.1 all-gather.15
  204.0 58.2 all-gather.25
  281.9 45.9 all-reduce.7
  396.8 33.0 all-gather.17
  441.2 144.4 reduce-scatter.1
  597.7 30.4 all-gather.19
  676.8 59.2 all-gather.27
  749.7 33.1 all-gather.21
  797.5 58.2 all-gather.29
  875.7 45.9 all-reduce.5
